TPU v7x, 512 devices: a whole 4x8x8 slice. The times are simulated.
512 devices in a mesh: fibre: 16 (over y, core), col: 32 (over x, z).
Axes of the slice: x: 4, y: 8, z: 8, core: 2. Of those that a mesh axis runs over, the one named last changes fastest.
Arguments:
- field: float32 [640, 160, 4096], P('fibre', None, 'col'), may hold values from -180 to 180, as said below
- start: float32 [640, 160], replicated, may hold values from -6 to 6
Outputs:
- basis: float32 [640, 160], replicated
- core: float32 [160, 160, 4096], P(None, 'fibre', 'col')
Inputs may be any that keep to these rules, and one draw needn't show every extreme that they name: `field`: entries are finite real values.
All inputs are finite; a program needn't handle non-finite values.
Results may differ from a plain program's by a relative error of at most 0.00016.
Values sent between devices are 32-bit elements; how exact they have to be, the bound alone decides.
No kernel may reach another device: no remote copies, remote signals or barrier semaphores. Data moves between devices by JAX's collectives and lax.ppermute only.
A program may use at most 64 MiB of HBM per device.

v0:
```python
import jax
import jax.numpy as jnp
from jax import lax
from jax.sharding import PartitionSpec as P

ITERS = 2


def subspace(gram, start):
    block = start
    for turn in range(ITERS):
        image = jnp.dot(
            gram, block, precision=lax.Precision.HIGHEST, preferred_element_type=jnp.float32
        )
        small = jnp.dot(
            image.T, image, precision=lax.Precision.HIGHEST, preferred_element_type=jnp.float32
        )
        factor = jnp.linalg.cholesky(small)
        block = lax.linalg.triangular_solve(
            factor, image, left_side=False, lower=True, transpose_a=True
        )
    return block


def shards(field, start):
    regrouped = lax.all_to_all(field, "fibre", split_axis=1, concat_axis=0, tiled=True)
    rows_all = regrouped.shape[0]
    unfolded = regrouped.reshape(rows_all, -1)
    local_gram = jnp.dot(
        unfolded, unfolded.T, precision=lax.Precision.HIGHEST, preferred_element_type=jnp.float32
    )
    gram = lax.psum(local_gram, ("fibre", "col"))
    basis = subspace(gram, start)
    core = jnp.dot(
        basis.T, unfolded, precision=lax.Precision.HIGHEST, preferred_element_type=jnp.float32
    )
    return (basis, core.reshape(basis.shape[1], regrouped.shape[1], regrouped.shape[2]))


def solution(mesh):
    in_specs = (P("fibre", None, "col"), P())
    out_specs = (P(), P(None, "fibre", "col"))
    return jax.shard_map(shards, mesh=mesh, in_specs=in_specs, out_specs=out_specs, check_vma=False)
```

profile of v0, /device:TPU:24, one launch (start us, length us, event | category | flops | bytes accessed | tf_op | source)
XLA Modules:
  0.0 505.7 jit_solution(5928552759673224963)
XLA Ops:
  7.2 0.0 copy-start
  7.2 0.0 all-reduce.5.cloned.1.call-start
  7.2 3.9 copy.7
  11.1 82.4 %all_to_all.15 = f32[40,160,128]{2,0,1:T(8,128)S(1)} all-to-all(f32[40,160,128]{2,0,1:T(8,128)S(1)} %copy.7), channel_id=1, replica_groups=mesh['fibre'=16,'col'=32] {'fibre'}, dimensions={1} | all-to-all | bytes 6553600 | tf_op jit(solution)/shard_map/all_to_all | solution.py:26
  93.5 0.8 copy.8
  94.2 0.0 copy-start.1
  94.3 2.3 copy-done.1
  96.6 10.5 %fusion = f32[640,640]{1,0:T(8,128)} fusion(f32[80,8,10,128]{3,2,1,0:T(8,128)S(1)} %bitcast.77), kind=kOutput, calls=%fused_computation.1 | convolution fusion | flops 6291456000 | bytes 4915200 | tf_op jit(solution)/shard_map/dot_general | solution.py:29
  107.1 0.0 all-reduce.5.cloned.1.call-update
  107.2 5.8 %copy.18 = f32[80,8,10,128]{3,1,2,0:T(8,128)} copy(f32[80,8,10,128]{3,2,1,0:T(8,128)} %bitcast.78) | data formatting | bytes 6553600
  112.9 4.7 copy.11
  117.7 270.5 %all-reduce.5.cloned.1.call-done = f32[640,640]{1,0:T(8,128)} async-done(((f32[640,640]{1,0:T(8,128)}), f32[640,640]{1,0:T(8,128)}) %all-reduce.5.cloned.1.call-update) | async-done | bytes 1638416 | tf_op jit(solution)/shard_map/psum | solution.py:32
  388.1 0.0 copy-done
  388.1 0.0 copy-start.2
  388.1 3.3 fusion.30
  391.5 0.6 fusion.31
  392.1 0.1 copy.9
  392.2 11.7 %cholesky.136 = f32[128,128]{1,0:T(8,128)S(1)} custom-call(f32[128,128]{1,0:T(8,128)S(1)} %cholesky.208), custom_call_target="Cholesky" | custom-call | tf_op jit(solution)/shard_map/jit(cholesky)/cholesky | solution.py:18
  404.0 9.8 %custom-call.13 = f32[1,128,128]{1,2,0:T(8,128)S(1)} custom-call(f32[1,128,128]{2,1,0:T(8,128)S(1)} %get-tuple-element.33), custom_call_target="InvertDiagBlocksLowerTriangular" | custom-call | tf_op jit(solution)/shard_map/jit(cholesky)/cholesky | solution.py:18
  413.8 0.2 constant_dynamic-update-slice_fusion.3
  414.0 0.2 convolution_subtract_fusion.3
  414.1 2.9 cholesky.156
  417.1 0.6 compare_reduce_fusion.2
  417.7 0.6 compare_reduce_fusion.3
  419.7 0.1 fusion.16
  419.8 19.9 %custom-call.14 = f32[2,128,128]{1,2,0:T(8,128)S(1)} custom-call(f32[2,128,128]{2,1,0:T(8,128)S(1)} %pad_maximum_fusion.1), custom_call_target="InvertDiagBlocksLowerTriangular" | custom-call | tf_op jit(solution)/shard_map/triangular_solve/custom-call.0 | solution.py:19
  439.7 0.5 fusion.11
  440.2 0.3 convolution_subtract_fusion.1
  440.5 0.3 fusion.26
  440.8 0.0 copy-done.2
  440.8 1.8 fusion.3
  442.6 0.6 fusion.32
  443.2 0.1 copy.10
  443.3 11.7 %cholesky.174 = f32[128,128]{1,0:T(8,128)S(1)} custom-call(f32[128,128]{1,0:T(8,128)S(1)} %cholesky.211), custom_call_target="Cholesky" | custom-call | tf_op jit(solution)/shard_map/jit(cholesky)/cholesky | solution.py:18
  455.1 9.8 %custom-call.15 = f32[1,128,128]{1,2,0:T(8,128)S(1)} custom-call(f32[1,128,128]{2,1,0:T(8,128)S(1)} %get-tuple-element.31), custom_call_target="InvertDiagBlocksLowerTriangular" | custom-call | tf_op jit(solution)/shard_map/jit(cholesky)/cholesky | solution.py:18
  464.9 0.2 constant_dynamic-update-slice_fusion.1
  465.1 0.2 convolution_subtract_fusion.2
  465.2 2.9 cholesky.194
  468.2 0.6 compare_reduce_fusion
  468.8 0.6 compare_reduce_fusion.1
  470.8 0.1 fusion.15
  470.9 19.9 %custom-call.16 = f32[2,128,128]{1,2,0:T(8,128)S(1)} custom-call(f32[2,128,128]{2,1,0:T(8,128)S(1)} %pad_maximum_fusion.2), custom_call_target="InvertDiagBlocksLowerTriangular" | custom-call | tf_op jit(solution)/shard_map/triangular_solve/custom-call.0 | solution.py:19
  490.9 0.5 fusion.9
  491.3 0.3 convolution_subtract_fusion
  491.6 0.3 fusion.23
  491.9 0.0 copy-start.3
  492.0 6.6 %fusion.7 = f32[160,10,128]{2,0,1:T(8,128)} fusion(f32[10,128,640]{2,1,0:T(8,128)} %bitcast.79, f32[640,160]{0,1:T(8,128)S(1)} %pad_maximum_fusion), kind=kOutput, calls=%fused_computation.13 | convolution fusion | flops 1572864000 | bytes 4505600 | tf_op jit(solution)/shard_map/dot_general | solution.py:34
  498.6 0.0 copy-done.3
  (20 shorter events, 0.3 us)
Async XLA Ops:
  7.2 381.0 %copy-start = (f32[640,160]{0,1:T(8,128)S(1)}, f32[640,160]{0,1:T(8,128)}, u32[]{:S(2)}) copy-start(f32[640,160]{0,1:T(8,128)} %param.6) | copy-start | bytes 1228804
  7.2 381.0 %all-reduce.5.cloned.1.call-start = ((), (), s32[]{:S(2)}) async-start(), calls=%async_computation.1 | async-start | bytes 3276800 | tf_op jit(solution)/shard_map/psum | solution.py:32
  94.2 2.3 copy-start.1
  388.1 52.6 %copy-start.2 = (f32[640,640]{1,0:T(8,128)S(1)}, f32[640,640]{1,0:T(8,128)}, u32[]{:S(2)}) copy-start(f32[640,640]{1,0:T(8,128)} %all-reduce.5.cloned.1.call-done) | copy-start | bytes 4915204
  491.9 6.6 %copy-start.3 = (f32[640,160]{0,1:T(8,128)}, f32[640,160]{0,1:T(8,128)S(1)}, u32[]{:S(2)}) copy-start(f32[640,160]{0,1:T(8,128)S(1)} %pad_maximum_fusion) | copy-start | bytes 1228804
Sparse Core Ops, SparseCore 0:
  107.3 280.8 all-reduce.4
where the time goes:
time: 508 us; the launch traced here: 506 us
  waiting for transfers between devices  270 us (53%)
  other arithmetic  91.7 us (18%)
  blocking collectives  82.4 us (16%)
  matrix products  26.1 us (5%)
  local copies, waits for them, and re-layouts  17.7 us (3%)
  between operations  17.2 us (3%)
    psum x1, waiting for transfers between devices, shards(): gram = lax.psum(local_gram, ('fibre', 'col'))  270 us
    all_to_all x1, blocking collectives, shards(): lax.all_to_all(field, 'fibre', split_axis=1, concat_axis=0, tiled=True)  82.4 us
    another operation x14, other arithmetic, subspace(): factor = jnp.linalg.cholesky(small)  51.6 us
    another operation x11, other arithmetic, subspace(): lax.linalg.triangular_solve(factor, image, left_side=False, lower=True, t...  40.1 us
    unnamed x10, local copies, waits for them, and re-layouts  12 us
    dot_general x1, matrix products, shards(): jnp.dot(unfolded, unfolded.T, precision=lax.Precision.HIGHEST, preferred_...  10.5 us
  transfers between devices with their start and end apart: 1, of which 1 were waited for; matrix products, arithmetic and copies ran while one was open for 2% of the time, Pallas kernels for 0%

commit v1 on v0

--- a/solution.py
+++ b/solution.py
@@ -1,9 +1,25 @@
+import functools
 import jax
 import jax.numpy as jnp
 from jax import lax
 from jax.sharding import PartitionSpec as P
 
 ITERS = 2
+
+
+def touch_the_tails(state, peer_axis):
+    return jnp.concatenate(
+        jax.lax.all_to_all(
+            jnp.stack(jnp.split(state, jax.lax.axis_size(peer_axis), axis=1)),
+            peer_axis,
+            split_axis=0,
+            concat_axis=0,
+        ),
+        axis=0,
+    )
+
+
+sizes_cut = functools.partial(touch_the_tails, peer_axis="fibre")
 
 
 def subspace(gram, start):
@@ -23,7 +39,7 @@
 
 
 def shards(field, start):
-    regrouped = lax.all_to_all(field, "fibre", split_axis=1, concat_axis=0, tiled=True)
+    regrouped = sizes_cut(field)
     rows_all = regrouped.shape[0]
     unfolded = regrouped.reshape(rows_all, -1)
     local_gram = jnp.dot(

time: 508 us -> 516 us (1.016); the launches traced: 506 us -> 506 us
    unnamed x10 -> x24, local copies, waits for them, and re-layouts: 12 us -> 9.05 us
where the time goes in v1:
time: 516 us; the launch traced here: 506 us
  waiting for transfers between devices  271 us (53%)
  other arithmetic  91.7 us (18%)
  blocking collectives  81.8 us (16%)
  matrix products  26.1 us (5%)
  local copies, waits for them, and re-layouts  18.5 us (4%)
  between operations  17.5 us (3%)
    psum x1, waiting for transfers between devices, shards(): gram = lax.psum(local_gram, ('fibre', 'col'))  271 us
    all_to_all x1, blocking collectives, touch_the_tails(): jax.lax.all_to_all(jnp.stack(jnp.split(state, jax.lax.axis_size(peer_axis...  81.8 us
    another operation x14, other arithmetic, subspace(): factor = jnp.linalg.cholesky(small)  51.6 us
    another operation x11, other arithmetic, subspace(): lax.linalg.triangular_solve(factor, image, left_side=False, lower=True, t...  40.1 us
    dot_general x1, matrix products, shards(): jnp.dot(unfolded, unfolded.T, precision=lax.Precision.HIGHEST, preferred_...  10.5 us
  transfers between devices with their start and end apart: 1, of which 1 were waited for; matrix products, arithmetic and copies ran while one was open for 2% of the time, Pallas kernels for 0%

profile of v1, /device:TPU:24, one launch (start us, length us, event | category | flops | bytes accessed | tf_op | source)
XLA Modules:
  0.0 506.3 jit_solution(15572728181197678426)
XLA Ops:
  7.2 3.6 fusion.46
  10.9 0.1 fusion.28
  11.0 0.1 fusion.27
  11.0 0.1 fusion.26
  11.1 0.1 fusion.25
  11.2 0.1 fusion.24
  11.4 0.1 fusion.21
  11.5 0.1 fusion.20
  11.5 0.1 fusion.19
  11.6 0.1 fusion.18
  12.0 81.8 %all_to_all.5 = f32[16,40,10,128]{3,1,2,0:T(8,128)S(1)} all-to-all(f32[16,40,10,128]{3,1,2,0:T(8,128)S(1)} %fusion.13), channel_id=1, replica_groups=mesh['fibre'=16,'col'=32] {'fibre'}, dimensions={0} | all-to-all | bytes 6553600 | tf_op jit(solution)/shard_map/all_to_all | solution.py:12
  93.8 0.8 copy.26
  94.6 2.3 copy-done.1
  96.9 10.5 %fusion = f32[640,640]{1,0:T(8,128)} fusion(f32[80,8,10,128]{3,2,1,0:T(8,128)S(1)} %bitcast.138), kind=kOutput, calls=%fused_computation.1 | convolution fusion | flops 6291456000 | bytes 4915200 | tf_op jit(solution)/shard_map/dot_general | solution.py:45
  107.5 5.8 %copy.100 = f32[80,8,10,128]{3,1,2,0:T(8,128)} copy(f32[80,8,10,128]{3,2,1,0:T(8,128)} %bitcast.139) | data formatting | bytes 6553600
  113.3 4.7 copy.29
  118.0 270.6 %all-reduce.5.cloned.1.call-done = f32[640,640]{1,0:T(8,128)} async-done(((f32[640,640]{1,0:T(8,128)}), f32[640,640]{1,0:T(8,128)}) %all-reduce.5.cloned.1.call-update) | async-done | bytes 1638416 | tf_op jit(solution)/shard_map/psum | solution.py:48
  388.6 3.3 fusion.47
  391.9 0.6 fusion.48
  392.5 0.1 copy.27
  392.7 11.7 %cholesky.136 = f32[128,128]{1,0:T(8,128)S(1)} custom-call(f32[128,128]{1,0:T(8,128)S(1)} %cholesky.208), custom_call_target="Cholesky" | custom-call | tf_op jit(solution)/shard_map/jit(cholesky)/cholesky | solution.py:34
  404.4 9.8 %custom-call.13 = f32[1,128,128]{1,2,0:T(8,128)S(1)} custom-call(f32[1,128,128]{2,1,0:T(8,128)S(1)} %get-tuple-element.49), custom_call_target="InvertDiagBlocksLowerTriangular" | custom-call | tf_op jit(solution)/shard_map/jit(cholesky)/cholesky | solution.py:34
  414.2 0.2 constant_dynamic-update-slice_fusion.3
  414.4 0.2 convolution_subtract_fusion.3
  414.6 2.9 cholesky.156
  417.5 0.6 compare_reduce_fusion.2
  418.2 0.6 compare_reduce_fusion.3
  420.1 0.1 fusion.32
  420.3 19.9 %custom-call.14 = f32[2,128,128]{1,2,0:T(8,128)S(1)} custom-call(f32[2,128,128]{2,1,0:T(8,128)S(1)} %pad_maximum_fusion.1), custom_call_target="InvertDiagBlocksLowerTriangular" | custom-call | tf_op jit(solution)/shard_map/triangular_solve/custom-call.0 | solution.py:35
  440.1 0.5 fusion.11
  440.6 0.3 convolution_subtract_fusion.1
  440.9 0.3 fusion.42
  441.2 1.8 fusion.3
  443.0 0.6 fusion.49
  443.6 0.1 copy.28
  443.8 11.7 %cholesky.174 = f32[128,128]{1,0:T(8,128)S(1)} custom-call(f32[128,128]{1,0:T(8,128)S(1)} %cholesky.211), custom_call_target="Cholesky" | custom-call | tf_op jit(solution)/shard_map/jit(cholesky)/cholesky | solution.py:34
  455.5 9.8 %custom-call.15 = f32[1,128,128]{1,2,0:T(8,128)S(1)} custom-call(f32[1,128,128]{2,1,0:T(8,128)S(1)} %get-tuple-element.47), custom_call_target="InvertDiagBlocksLowerTriangular" | custom-call | tf_op jit(solution)/shard_map/jit(cholesky)/cholesky | solution.py:34
  465.3 0.2 constant_dynamic-update-slice_fusion.1
  465.5 0.2 convolution_subtract_fusion.2
  465.7 2.9 cholesky.194
  468.6 0.6 compare_reduce_fusion
  469.3 0.6 compare_reduce_fusion.1
  471.2 0.1 fusion.31
  471.4 19.9 %custom-call.16 = f32[2,128,128]{1,2,0:T(8,128)S(1)} custom-call(f32[2,128,128]{2,1,0:T(8,128)S(1)} %pad_maximum_fusion.2), custom_call_target="InvertDiagBlocksLowerTriangular" | custom-call | tf_op jit(solution)/shard_map/triangular_solve/custom-call.0 | solution.py:35
  491.3 0.5 fusion.9
  491.8 0.3 convolution_subtract_fusion
  492.1 0.3 fusion.39
  492.4 6.6 %fusion.7 = f32[160,10,128]{2,0,1:T(8,128)} fusion(f32[10,128,640]{2,1,0:T(8,128)} %bitcast.140, f32[640,160]{0,1:T(8,128)S(1)} %pad_maximum_fusion), kind=kOutput, calls=%fused_computation.13 | convolution fusion | flops 1572864000 | bytes 4505600 | tf_op jit(solution)/shard_map/dot_general | solution.py:50
  (36 shorter events, 0.9 us)
Async XLA Ops:
  7.2 381.4 %copy-start = (f32[640,160]{0,1:T(8,128)S(1)}, f32[640,160]{0,1:T(8,128)}, u32[]{:S(2)}) copy-start(f32[640,160]{0,1:T(8,128)} %param.6) | copy-start | bytes 1228804
  7.2 381.4 %all-reduce.5.cloned.1.call-start = ((), (), s32[]{:S(2)}) async-start(), calls=%async_computation.1 | async-start | bytes 3276800 | tf_op jit(solution)/shard_map/psum | solution.py:48
  94.6 2.3 copy-start.1
  388.6 52.6 %copy-start.2 = (f32[640,640]{1,0:T(8,128)S(1)}, f32[640,640]{1,0:T(8,128)}, u32[]{:S(2)}) copy-start(f32[640,640]{1,0:T(8,128)} %all-reduce.5.cloned.1.call-done) | copy-start | bytes 4915204
  492.4 6.6 %copy-start.3 = (f32[640,160]{0,1:T(8,128)}, f32[640,160]{0,1:T(8,128)S(1)}, u32[]{:S(2)}) copy-start(f32[640,160]{0,1:T(8,128)S(1)} %pad_maximum_fusion) | copy-start | bytes 1228804
Sparse Core Ops, SparseCore 0:
  107.6 280.9 all-reduce.4
